TPU v7x, 32 devices: a whole 2x2x4 slice. The times are simulated.
32 devices in a mesh: prow: 8 (over y, x, core), pcol: 4 (over z).
Axes of the slice: x: 2, y: 2, z: 4, core: 2. Of those that a mesh axis runs over, the one named last changes fastest.
Arguments:
- panel: float32 [32768, 512], P('prow', 'pcol'), may hold values from -0.08 to 0.08
- slab: float32 [32768, 2048], P('prow', 'pcol'), may hold values from -6 to 6
- pivots: int32 [512], replicated, may hold values from 512 to 32767, as said below
- diag_inverse: float32 [512, 512], replicated, as said below
Outputs:
- updated: float32 [32768, 2048], P('prow', 'pcol')
Inputs may be any that keep to these rules, and one draw needn't show every extreme that they name: `pivots`: 512 distinct row indices, each below the diagonal block; their owners along prow are uneven. `diag_inverse`: unit lower triangular.
All inputs are finite; a program needn't handle non-finite values.
Results may differ from a plain program's by a relative error of at most 0.000053.
Values sent between devices are 32-bit elements; how exact they have to be, the bound alone decides.
No kernel may reach another device: no remote copies, remote signals or barrier semaphores. Data moves between devices by JAX's collectives and lax.ppermute only.
A program may use at most 128 MiB of HBM per device.

v0:
```python
import jax
import jax.numpy as jnp
from jax import lax
from jax.sharding import PartitionSpec as P


def from_root(value, axis, source):
    kept = jnp.where(lax.axis_index(axis) == source, value, 0).astype(value.dtype)
    return lax.psum(kept, axis)


def shards(panel, slab, pivots, diag_inverse):
    rows_here = slab.shape[0]
    width_here = slab.shape[1]
    block_size = diag_inverse.shape[0]
    first_row = lax.axis_index("prow") * rows_here
    local_row = pivots - first_row
    owned = (local_row >= 0) & (local_row < rows_here)
    safe_row = jnp.clip(local_row, 0, rows_here - 1)
    picked = jnp.where(owned[:, None], slab[safe_row], 0.0)
    top_block = lax.psum(picked, "prow")
    upper = jnp.dot(
        diag_inverse, top_block, precision=lax.Precision.HIGHEST, preferred_element_type=jnp.float32
    )
    old_top = from_root(slab[:block_size], "prow", 0)
    target_row = jnp.where(owned, local_row, rows_here)
    swapped = slab.at[target_row].set(old_top, mode="drop")
    product = jnp.dot(
        lax.all_gather(panel, "pcol", axis=1, tiled=True),
        upper,
        precision=lax.Precision.HIGHEST,
        preferred_element_type=jnp.float32,
    )
    updated = swapped - product
    global_row = first_row + jnp.arange(rows_here, dtype=jnp.int32)
    upper_padded = jnp.concatenate(
        [upper, jnp.zeros((rows_here - block_size, width_here), jnp.float32)], axis=0
    )
    return jnp.where((global_row < block_size)[:, None], upper_padded, updated)


def solution(mesh):
    in_specs = (P("prow", "pcol"), P("prow", "pcol"), P(), P())
    out_specs = P("prow", "pcol")
    return jax.shard_map(shards, mesh=mesh, in_specs=in_specs, out_specs=out_specs, check_vma=False)
```

profile of v0, /device:TPU:0, one launch (start us, length us, event | category | flops | bytes accessed | tf_op | source)
XLA Modules:
  0.0 213.0 jit_solution(16660323267572027275)
XLA Ops:
  7.4 0.0 copy-start
  7.4 0.0 copy-start.2
  7.4 0.0 all-reduce.4.cloned.1.call-start
  7.4 7.9 %copy.11 = f32[4096,512]{1,0:T(8,128)} copy(f32[4096,512]{1,0:T(8,128)} %param.5) | data formatting | bytes 16777216
  15.2 0.0 copy-done.2
  15.3 5.4 %gather_fusion = f32[512,512]{1,0:T(8,128)S(1)} fusion(f32[4096,512]{1,0:T(8,128)} %copy.11, s32[1024]{0:T(1024)S(1)} %pad_clamp_fusion), kind=kCustom, calls=%fused_computation | custom fusion | bytes 2099200 | tf_op jit(solution)/shard_map/gather | solution.py:20
  20.7 2.8 %slice_select_fusion = (f32[512,512]{1,0:T(8,128)}, f32[512,512]{1,0:T(8,128)}) fusion(f32[4096,512]{1,0:T(8,128)} %copy.11, pred[]{:T(512)S(6)} %eq.3, f32[512,512]{1,0:T(8,128)S(1)} %gather_fusion, pred[512]{0:T(512)(128)(4,1)S(1)} %compare_and_fusion), kind=kLoop, calls=%fused_computation.4 | loop fusion | flops 524288 | bytes 4194817 | tf_op jit(solution)/shard_map/jit(_where)/select_n | solution.py:8
  23.5 0.0 all-reduce.4.cloned.1.call-update
  23.5 0.0 all-gather.2.cloned.1.call-start
  23.5 0.5 all-gather.2.cloned.1.call-update
  24.1 63.8 %all-reduce.4.cloned.1.call-done = (f32[512,512]{1,0:T(8,128)}, f32[512,512]{1,0:T(8,128)}) async-done(((f32[512,512]{1,0:T(8,128)}, f32[512,512]{1,0:T(8,128)}), (f32[512,512]{1,0:T(8,128)}, f32[512,512]{1,0:T(8,128)})) %all-reduce.4.cloned.1.call-update) | async-done | bytes 2097168 | tf_op jit(solution)/shard_map/psum | solution.py:9
  87.9 9.7 %scatter_fusion = f32[4096,512]{1,0:T(8,128)} fusion(f32[4096,512]{1,0:T(8,128)} %copy.11, s32[512]{0:T(512)S(1)} %get-tuple-element.8, f32[512,512]{1,0:T(8,128)} %get-tuple-element.5), kind=kCustom, calls=%fused_computation.1 | custom fusion | bytes 3147776 | tf_op jit(solution)/shard_map/scatter | solution.py:27
  97.6 0.0 copy-start.1
  97.6 9.0 %copy.5 = f32[4096,512]{0,1:T(8,128)} copy(f32[4096,512]{1,0:T(8,128)} %scatter_fusion) | data formatting | bytes 16777216 | tf_op jit(solution)/shard_map/scatter | solution.py:27
  106.7 0.0 copy-done
  106.7 0.0 copy-done.1
  106.7 3.5 %fusion.1 = f32[512,512]{1,0:T(8,128)S(1)} fusion(f32[512,512]{1,0:T(8,128)S(1)} %copy-done.1, f32[512,512]{1,0:T(8,128)S(1)} %copy-done), kind=kOutput, calls=%fused_computation.11 | convolution fusion | flops 1610612736 | bytes 3145728 | tf_op jit(solution)/shard_map/dot_general | solution.py:22
  110.1 67.1 %all-gather.2.cloned.1.call-done = f32[4096,512]{1,0:T(8,128)} async-done(((f32[4096,128]{1,0:T(8,128)}), f32[4096,512]{1,0:T(8,128)}) %all-gather.2.cloned.1.call-update) | async-done | bytes 8388624 | tf_op jit(solution)/shard_map/all_gather | solution.py:29
  177.2 19.4 %fusion = f32[4096,512]{0,1:T(8,128)} fusion(f32[4096,512]{0,1:T(8,128)} %copy.5, f32[512,512]{0,1:T(8,128)S(1)} %bitcast.9, f32[512,512]{1,0:T(8,128)S(1)} %fusion.1, f32[4096,512]{1,0:T(8,128)} %all-gather.2.cloned.1.call-done, pred[4096]{0:T(1024)(128)(4,1)S(1)} %add_compare_fusion), kind=kOutput, calls=%fused_computation.3 | convolution fusion | flops 12889096192 | bytes 27267072 | tf_op jit(solution)/shard_map/dot_general | solution.py:28
  196.6 8.9 %copy.6 = f32[4096,512]{1,0:T(8,128)} copy(f32[4096,512]{0,1:T(8,128)} %fusion) | data formatting | bytes 16777216 | tf_op jit(solution)/shard_map/jit(_where)/select_n | solution.py:39
  (4 shorter events, 0.0 us)
Async XLA Ops:
  7.4 99.3 %copy-start = (f32[512,512]{1,0:T(8,128)S(1)}, f32[512,512]{1,0:T(8,128)}, u32[]{:S(2)}) copy-start(f32[512,512]{1,0:T(8,128)} %param.7) | copy-start | bytes 3145732
  7.4 7.9 %copy-start.2 = (s32[512]{0:T(512)S(1)}, s32[512]{0:T(512)}, u32[]{:S(2)}) copy-start(s32[512]{0:T(512)} %param.6) | copy-start | bytes 6148
  7.4 80.5 %all-reduce.4.cloned.1.call-start = ((), (), s32[]{:S(2)}) async-start(), calls=%async_computation.1 | async-start | bytes 4194304 | tf_op jit(solution)/shard_map/psum | solution.py:9
  23.5 153.7 %all-gather.2.cloned.1.call-start = ((), (), s32[]{:S(2)}) async-start(), calls=%async_computation | async-start | bytes 10485760 | tf_op jit(solution)/shard_map/all_gather | solution.py:29
  97.6 9.1 %copy-start.1 = (f32[512,512]{1,0:T(8,128)S(1)}, f32[512,512]{1,0:T(8,128)}, u32[]{:S(2)}) copy-start(f32[512,512]{1,0:T(8,128)} %get-tuple-element.6) | copy-start | bytes 3145732
Sparse Core Ops, SparseCore 0:
  23.6 64.2 all-reduce.3
Sparse Core Ops, SparseCore 1:
  25.5 151.6 all-gather.1
where the time goes:
time: 214 us; the launch traced here: 213 us
  waiting for transfers between devices  131 us (61%)
  local copies, waits for them, and re-layouts  41 us (19%)
  matrix products  22.8 us (11%)
  between operations  14.9 us (7%)
  other arithmetic  2.79 us (1%)
    all_gather x1, waiting for transfers between devices, shards(): lax.all_gather(panel, 'pcol', axis=1, tiled=True)  67.1 us
    psum x1, waiting for transfers between devices, from_root(): return lax.psum(kept, axis)  63.8 us
    dot_general x1, matrix products, shards(): jnp.dot(lax.all_gather(panel, 'pcol', axis=1, tiled=True), upper, precisi...  19.4 us
    scatter x2, local copies, waits for them, and re-layouts, shards(): swapped = slab.at[target_row].set(old_top, mode='drop')  18.8 us
    select_n x1, local copies, waits for them, and re-layouts, shards(): return jnp.where((global_row < block_size)[:, None], upper_padded, updated)  8.94 us
    unnamed x7, local copies, waits for them, and re-layouts  7.87 us
    gather x1, local copies, waits for them, and re-layouts, shards(): picked = jnp.where(owned[:, None], slab[safe_row], 0.0)  5.41 us
  transfers between devices with their start and end apart: 2, of which 2 were waited for; matrix products, arithmetic and copies ran while one was open for 10% of the time, Pallas kernels for 0%

commit v1 on v0

--- a/solution.py
+++ b/solution.py
@@ -6,7 +6,7 @@
 
 def from_root(value, axis, source):
     kept = jnp.where(lax.axis_index(axis) == source, value, 0).astype(value.dtype)
-    return lax.psum(kept, axis)
+    return jnp.sum(lax.all_gather(kept, axis), axis=0)
 
 
 def shards(panel, slab, pivots, diag_inverse):

time: 214 us -> 322 us (1.50)
  waiting for transfers between devices: 131 us -> 236 us
  other arithmetic: 2.79 us -> 7.99 us
    all_gather x1, waiting for transfers between devices: 67.1 us -> 128 us  [shards(): lax.all_gather(panel, 'pcol', axis=1, tiled=True)]
    all_gather x0 -> x1, waiting for transfers between devices: none -> 50.7 us  [from_root(): return jnp.sum(lax.all_gather(kept, axis), axis=0)]
    psum x1, waiting for transfers between devices: 63.8 us -> 56.3 us  [shards(): top_block = lax.psum(picked, 'prow')]
    reduce_sum x0 -> x1, other arithmetic: none -> 4.49 us  [from_root(): return jnp.sum(lax.all_gather(kept, axis), axis=0)]
  transfers between devices with their start and end apart: 2 -> 3, of which waited for: 2 -> 3; matrix products, arithmetic and copies ran while one was open for 10% -> 9% of each run, Pallas kernels for 0% -> 0%
where the time goes in v1:
time: 322 us; the launch traced here: 321 us
  waiting for transfers between devices  236 us (73%)
  local copies, waits for them, and re-layouts  40.2 us (12%)
  matrix products  24 us (7%)
  between operations  13.2 us (4%)
  other arithmetic  7.99 us (2%)
    all_gather x1, waiting for transfers between devices, shards(): lax.all_gather(panel, 'pcol', axis=1, tiled=True)  128 us
    psum x1, waiting for transfers between devices, shards(): top_block = lax.psum(picked, 'prow')  56.3 us
    all_gather x1, waiting for transfers between devices, from_root(): return jnp.sum(lax.all_gather(kept, axis), axis=0)  50.7 us
    dot_general x1, matrix products, shards(): jnp.dot(lax.all_gather(panel, 'pcol', axis=1, tiled=True), upper, precisi...  19.3 us
    scatter x2, local copies, waits for them, and re-layouts, shards(): swapped = slab.at[target_row].set(old_top, mode='drop')  18 us
    select_n x1, local copies, waits for them, and re-layouts, shards(): return jnp.where((global_row < block_size)[:, None], upper_padded, updated)  8.94 us
    unnamed x7, local copies, waits for them, and re-layouts  7.87 us
  transfers between devices with their start and end apart: 3, of which 3 were waited for; matrix products, arithmetic and copies ran while one was open for 9% of the time, Pallas kernels for 0%

profile of v1, /device:TPU:0, one launch (start us, length us, event | category | flops | bytes accessed | tf_op | source)
XLA Modules:
  0.0 321.4 jit_solution(14522470752486539905)
XLA Ops:
  6.5 0.0 copy-start
  6.5 0.0 copy-start.2
  6.5 0.0 all-reduce.3.cloned.1.call-start
  6.5 7.9 %copy.10 = f32[4096,512]{1,0:T(8,128)} copy(f32[4096,512]{1,0:T(8,128)} %param.5) | data formatting | bytes 16777216
  14.4 0.0 copy-done.2
  14.4 5.4 %gather_fusion = f32[512,512]{1,0:T(8,128)S(1)} fusion(f32[4096,512]{1,0:T(8,128)} %copy.10, s32[1024]{0:T(1024)S(1)} %pad_clamp_fusion), kind=kCustom, calls=%fused_computation | custom fusion | bytes 2099200 | tf_op jit(solution)/shard_map/gather | solution.py:20
  19.9 1.1 broadcast_select_fusion
  21.0 0.0 all-reduce.3.cloned.1.call-update
  21.0 0.0 all-gather.6.cloned.1.call-start
  21.1 2.3 slice_select_fusion
  23.4 0.0 all-gather.6.cloned.1.call-update
  23.4 0.0 all-gather.4.cloned.1.call-start
  23.5 0.7 all-gather.4.cloned.1.call-update
  24.2 56.3 %all-reduce.3.cloned.1.call-done = f32[512,512]{1,0:T(8,128)} async-done(((f32[512,512]{1,0:T(8,128)}), f32[512,512]{1,0:T(8,128)}) %all-reduce.3.cloned.1.call-update) | async-done | bytes 1048592 | tf_op jit(solution)/shard_map/psum | solution.py:21
  80.5 0.0 copy-done
  80.5 4.7 %fusion.1 = f32[512,512]{1,0:T(8,128)S(1)} fusion(f32[512,512]{1,0:T(8,128)} %all-reduce.3.cloned.1.call-done, f32[512,512]{1,0:T(8,128)S(1)} %copy-done), kind=kOutput, calls=%fused_computation.11 | convolution fusion | flops 1610612736 | bytes 3145728 | tf_op jit(solution)/shard_map/dot_general | solution.py:22
  85.2 50.7 %all-gather.6.cloned.1.call-done = f32[4096,512]{1,0:T(8,128)} async-done(((f32[512,512]{1,0:T(8,128)}), f32[4096,512]{1,0:T(8,128)}) %all-gather.6.cloned.1.call-update) | async-done | bytes 8388624 | tf_op jit(solution)/shard_map/all_gather | solution.py:9
  135.8 4.5 %reduce_sum.9 = f32[512,512]{1,0:T(8,128)S(1)} reduce(f32[8,512,512]{2,1,0:T(8,128)} %bitcast.11, f32[]{:T(128)} %constant.6.clone.1), dimensions={0}, to_apply=%region_1.2 | reduce | flops 1835008 | bytes 9437188 | tf_op jit(solution)/shard_map/reduce_sum | solution.py:9
  140.3 9.0 %scatter_fusion = f32[4096,512]{1,0:T(8,128)} fusion(f32[4096,512]{1,0:T(8,128)} %copy.10, s32[512]{0:T(512)S(1)} %get-tuple-element.6, f32[512,512]{1,0:T(8,128)S(1)} %reduce_sum.9), kind=kCustom, calls=%fused_computation.1 | custom fusion | bytes 3147776 | tf_op jit(solution)/shard_map/scatter | solution.py:27
  149.3 9.0 %copy.5 = f32[4096,512]{0,1:T(8,128)} copy(f32[4096,512]{1,0:T(8,128)} %scatter_fusion) | data formatting | bytes 16777216 | tf_op jit(solution)/shard_map/scatter | solution.py:27
  158.3 128.3 %all-gather.4.cloned.1.call-done = f32[4096,512]{1,0:T(8,128)} async-done(((f32[4096,128]{1,0:T(8,128)}), f32[4096,512]{1,0:T(8,128)}) %all-gather.4.cloned.1.call-update) | async-done | bytes 8388624 | tf_op jit(solution)/shard_map/all_gather | solution.py:29
  286.6 0.0 copy-start.1
  286.6 19.3 %fusion = f32[4096,512]{0,1:T(8,128)} fusion(f32[4096,512]{0,1:T(8,128)} %copy.5, f32[512,512]{0,1:T(8,128)S(1)} %bitcast.10, f32[512,512]{1,0:T(8,128)S(1)} %fusion.1, f32[4096,512]{1,0:T(8,128)} %all-gather.4.cloned.1.call-done, pred[4096]{0:T(1024)(128)(4,1)S(1)} %add_compare_fusion), kind=kOutput, calls=%fused_computation.3 | convolution fusion | flops 12889096192 | bytes 27267072 | tf_op jit(solution)/shard_map/dot_general | solution.py:28
  305.9 8.9 %copy.6 = f32[4096,512]{1,0:T(8,128)} copy(f32[4096,512]{0,1:T(8,128)} %fusion) | data formatting | bytes 16777216 | tf_op jit(solution)/shard_map/jit(_where)/select_n | solution.py:39
  314.8 0.0 copy-done.1
  (4 shorter events, 0.0 us)
Async XLA Ops:
  6.5 73.9 %copy-start = (f32[512,512]{1,0:T(8,128)S(1)}, f32[512,512]{1,0:T(8,128)}, u32[]{:S(2)}) copy-start(f32[512,512]{1,0:T(8,128)} %param.7) | copy-start | bytes 3145732
  6.5 7.9 %copy-start.2 = (s32[512]{0:T(512)S(1)}, s32[512]{0:T(512)}, u32[]{:S(2)}) copy-start(s32[512]{0:T(512)} %param.6) | copy-start | bytes 6148
  6.5 73.9 %all-reduce.3.cloned.1.call-start = ((), (), s32[]{:S(2)}) async-start(), calls=%async_computation | async-start | bytes 2097152 | tf_op jit(solution)/shard_map/psum | solution.py:21
  21.0 114.8 %all-gather.6.cloned.1.call-start = ((), (), s32[]{:S(2)}) async-start(), calls=%async_computation.2 | async-start | bytes 9437184 | tf_op jit(solution)/shard_map/all_gather | solution.py:9
  23.4 263.1 %all-gather.4.cloned.1.call-start = ((), (), s32[]{:S(2)}) async-start(), calls=%async_computation.1 | async-start | bytes 10485760 | tf_op jit(solution)/shard_map/all_gather | solution.py:29
  286.6 28.3 %copy-start.1 = (f32[512,512]{1,0:T(8,128)S(1)}, f32[512,512]{1,0:T(8,128)}, u32[]{:S(2)}) copy-start(f32[512,512]{1,0:T(8,128)} %param.7) | copy-start | bytes 3145732
Sparse Core Ops, SparseCore 0:
  21.1 59.2 all-reduce.2
  82.4 53.4 all-gather.5
  137.4 149.1 all-gather.3
